TPU v7x, 128 devices: a whole 4x4x4 slice. The times are simulated.
128 devices in a mesh: row: 8 (over x, y_hi), col: 16 (over z, y_lo, core).
Axes of the slice: x: 4, y: 4 (y_hi: 2, y_lo: 2; y = y_hi * 2 + y_lo), z: 4, core: 2. Of those that a mesh axis runs over, the one named last changes fastest.
Arguments:
- density: float32 [5120, 5120], P('row', 'col'), as said below
- pattern: int32 [80, 80], P('row', 'col'), may hold values from 0 to 1, as said below
- weights: float32 [5120], P('row'), may hold values from 0.5 to 5
Outputs:
- purified: float32 [5120, 5120], P('row', 'col')
- checks: float32 [2, 5120], P(None, 'col')
Inputs may be any that keep to these rules, and one draw needn't show every extreme that they name: pattern is symmetric, and every block with |a - b| <= 2 is nonzero; the number of nonzero blocks differs strongly between block rows. density is symmetric and zero outside the blocks that pattern marks.
All inputs are finite; a program needn't handle non-finite values.
Results may differ from a plain program's by a relative error of at most 0.00012.
Values sent between devices are 32-bit elements; how exact they have to be, the bound alone decides.
A program may use at most 64 MiB of HBM per device.

v0:
```python
import jax
import jax.numpy as jnp
from jax import lax
from jax.sharding import PartitionSpec as P

BLK = 64


def full_dot(first, second):
    return jnp.dot(
        first, second, precision=lax.Precision.HIGHEST, preferred_element_type=jnp.float32
    )


def expand_mask(pattern):
    return jnp.repeat(jnp.repeat(pattern.astype(jnp.float32), BLK, axis=0), BLK, axis=1)


def multiply(left_tile, column, weight_row):
    partial_row = full_dot(weight_row, left_tile)
    result = full_dot(lax.all_gather(left_tile, "col", axis=1, tiled=True), column)
    summed = lax.psum(partial_row, "row")
    full_check = lax.all_gather(summed, "col", axis=1, tiled=True)
    check_row = full_dot(full_check, column)
    return (result, check_row)


def body(density, pattern, weights):
    block_mask = expand_mask(pattern)
    current = density
    weight_row = weights[None, :]
    checks = []
    column = lax.all_gather(current, "row", axis=0, tiled=True)
    square, first_check = multiply(current, column, weight_row)
    square = block_mask * square
    cube_term, second_check = multiply(square, column, weight_row)
    cube_term = block_mask * cube_term
    current = 3.0 * square - 2.0 * cube_term
    checks.append(first_check)
    checks.append(second_check)
    return (current, jnp.concatenate(checks, axis=0))


def solution(mesh):
    in_specs = (P("row", "col"), P("row", "col"), P("row"))
    out_specs = (P("row", "col"), P(None, "col"))
    return jax.shard_map(body, mesh=mesh, in_specs=in_specs, out_specs=out_specs, check_vma=False)
```

profile of v0, /device:TPU:0, one launch (start us, length us, event | category | flops | bytes accessed | tf_op | source)
XLA Modules:
  0.0 325.3 jit_solution(1333417447258999586)
XLA Ops:
  7.2 0.0 all-gather.6.cloned.1.call-start
  7.2 0.7 all-gather.6.cloned.1.call-update
  7.9 0.0 all-gather.4.cloned.1.call-start
  7.9 0.7 all-gather.4.cloned.1.call-update
  8.6 0.0 all-gather.8.cloned.1.call-start
  8.7 0.7 convert_element_type.3
  9.4 0.1 broadcast_in_dim.7
  9.5 0.1 reshape.24
  9.5 94.3 %all-gather.6.cloned.1.call-done = f32[5120,320]{0,1:T(8,128)} async-done(((f32[640,320]{0,1:T(8,128)}), f32[5120,320]{0,1:T(8,128)}) %all-gather.6.cloned.1.call-update) | async-done | bytes 6553616 | tf_op jit(solution)/shard_map/all_gather | solution.py:33
  103.9 73.9 %all-gather.4.cloned.1.call-done = f32[640,5120]{0,1:T(8,128)} async-done(((f32[640,320]{0,1:T(8,128)}), f32[640,5120]{0,1:T(8,128)}) %all-gather.4.cloned.1.call-update) | async-done | bytes 13107216 | tf_op jit(solution)/shard_map/all_gather | solution.py:21
  177.8 0.1 broadcast_in_dim.8
  177.9 0.0 copy-start.2
  177.9 0.0 copy-start.3
  177.9 0.0 copy-start.1
  177.9 20.3 %convolution_multiply_fusion.1 = f32[640,320]{0,1:T(8,128)} fusion(f32[640,320]{0,1:T(8,128)S(1)} %bitcast.18, f32[640,5120]{0,1:T(8,128)} %all-gather.4.cloned.1.call-done, f32[5120,320]{0,1:T(8,128)} %all-gather.6.cloned.1.call-done), kind=kOutput, calls=%fused_computation.1 | convolution fusion | flops 12583116800 | bytes 21299200 | tf_op jit(solution)/shard_map/dot_general | solution.py:10
  198.2 0.0 all-gather.8.cloned.1.call-update
  198.3 0.0 copy-done.2
  198.3 0.0 copy-done.3
  198.3 0.6 dynamic-slice
  199.5 0.0 copy-done.1
  199.5 0.8 fusion.2
  200.3 2.0 fusion.4
  202.3 24.4 %all-reduce.3 = (f32[1,320]{1,0:T(1,128)S(1)}, f32[1,320]{1,0:T(1,128)S(1)}) all-reduce(f32[1,320]{1,0:T(1,128)S(1)} %fusion.4, f32[1,320]{1,0:T(1,128)S(1)} %fusion.2), channel_id=1, replica_groups=mesh['row'=8,'col'=16] {'row'}, use_global_device_ids=true, to_apply=%region_1.0 | all-reduce | flops 640 | bytes 5120 | tf_op jit(solution)/shard_map/psum | solution.py:22
  226.7 0.3 dynamic-update-slice
  227.0 0.3 dynamic-update-slice.1
  227.3 55.8 %all-reduce.2 = (f32[5120]{0:T(1024)S(1)}, f32[5120]{0:T(1024)S(1)}) all-reduce(f32[5120]{0:T(1024)S(1)} %dynamic-update-slice.1, f32[5120]{0:T(1024)S(1)} %dynamic-update-slice), channel_id=1, replica_groups=mesh['row'=8,'col'=16] {'col'}, use_global_device_ids=true, to_apply=%add.1 | all-reduce | flops 10240 | bytes 81920 | tf_op jit(solution)/shard_map/reshape.10
  283.1 0.0 copy-start
  283.1 7.4 %fusion.3 = f32[1,320]{1,0:T(1,128)S(1)} fusion(f32[5120,1]{0,1:T(1,128)S(1)} %bitcast.21, f32[5120,320]{0,1:T(8,128)} %all-gather.6.cloned.1.call-done), kind=kOutput, calls=%fused_computation.6 | convolution fusion | flops 19660800 | bytes 6575360 | tf_op jit(solution)/shard_map/dot_general | solution.py:10
  290.5 7.3 %fusion.5 = f32[1,320]{1,0:T(1,128)S(1)} fusion(f32[5120,1]{0,1:T(1,128)S(1)} %bitcast.20, f32[5120,320]{0,1:T(8,128)} %all-gather.6.cloned.1.call-done), kind=kOutput, calls=%fused_computation.8 | convolution fusion | flops 19660800 | bytes 6575360 | tf_op jit(solution)/shard_map/dot_general | solution.py:10
  297.8 0.6 pad_maximum_fusion
  298.4 0.0 all-gather.8.cloned.1.call-done
  298.4 0.0 copy-done
  298.4 20.3 %fusion.1 = f32[640,320]{0,1:T(8,128)} fusion(f32[640,320]{0,1:T(8,128)S(1)} %bitcast.19, f32[640,5120]{0,1:T(8,128)} %all-gather.8.cloned.1.call-done, f32[5120,320]{0,1:T(8,128)} %all-gather.6.cloned.1.call-done, f32[640,320]{0,1:T(8,128)S(1)} %copy-done), kind=kOutput, calls=%fused_computation.3 | convolution fusion | flops 12583731200 | bytes 22118400 | tf_op jit(solution)/shard_map/dot_general | solution.py:10
  (5 shorter events, 0.1 us)
Async XLA Ops:
  7.2 96.7 %all-gather.6.cloned.1.call-start = ((), (), s32[]{:S(2)}) async-start(), calls=%async_computation.1 | async-start | bytes 7372800 | tf_op jit(solution)/shard_map/all_gather | solution.py:33
  7.9 169.9 %all-gather.4.cloned.1.call-start = ((), (), s32[]{:S(2)}) async-start(), calls=%async_computation | async-start | bytes 13926400 | tf_op jit(solution)/shard_map/all_gather | solution.py:21
  8.6 289.8 %all-gather.8.cloned.1.call-start = ((), (), s32[]{:S(2)}) async-start(), calls=%async_computation.2 | async-start | bytes 13926400 | tf_op jit(solution)/shard_map/all_gather | solution.py:21
  177.9 20.4 %copy-start.2 = (f32[640]{0:T(1024)S(1)}, f32[640]{0:T(1024)}, u32[]{:S(2)}) copy-start(f32[640]{0:T(1024)} %param.5) | copy-start | bytes 7684
  177.9 20.4 %copy-start.3 = (u32[128]{0:T(128)S(1)}, u32[128]{0:T(128)}, u32[]{:S(2)}) copy-start(u32[128]{0:T(128)} %constant.7) | copy-start | bytes 1540
  177.9 21.7 %copy-start.1 = (f32[640,320]{0,1:T(8,128)S(1)}, f32[640,320]{0,1:T(8,128)}, u32[]{:S(2)}) copy-start(f32[640,320]{0,1:T(8,128)} %param.3) | copy-start | bytes 2457604
  283.1 15.4 %copy-start = (f32[640,320]{0,1:T(8,128)S(1)}, f32[640,320]{0,1:T(8,128)}, u32[]{:S(2)}) copy-start(f32[640,320]{0,1:T(8,128)} %convolution_multiply_fusion.1) | copy-start | bytes 2457604
Sparse Core Ops, SparseCore 0:
  10.3 93.5 all-gather.5
  105.6 72.1 all-gather.3
  198.4 76.7 all-gather.7
where the time goes:
time: 325 us
  waiting for transfers between devices  170 us (52%)
  blocking collectives  80.2 us (25%)
  matrix products  58.1 us (18%)
  between operations  14.5 us (4%)
    all_gather x1, waiting for transfers between devices, body(): column = lax.all_gather(current, 'row', axis=0, tiled=True)  94.3 us
    all_gather x2, waiting for transfers between devices, multiply(): lax.all_gather(left_tile, 'col', axis=1, tiled=True)  73.9 us
    dot_general x6, matrix products, full_dot(): jnp.dot(first, second, precision=lax.Precision.HIGHEST, preferred_element...  58.1 us
    another operation x1, blocking collectives  55.8 us
    psum x1, blocking collectives, multiply(): summed = lax.psum(partial_row, 'row')  24.4 us
  transfers between devices with their start and end apart: 3, of which 2 were waited for; matrix products, arithmetic and copies ran while one was open for 6% of the time, Pallas kernels for 0%

commit v1 on v0

--- a/solution.py
+++ b/solution.py
@@ -19,7 +19,7 @@
 def multiply(left_tile, column, weight_row):
     partial_row = full_dot(weight_row, left_tile)
     result = full_dot(lax.all_gather(left_tile, "col", axis=1, tiled=True), column)
-    summed = lax.psum(partial_row, "row")
+    summed = jnp.sum(lax.all_gather(partial_row, "row"), axis=0)
     full_check = lax.all_gather(summed, "col", axis=1, tiled=True)
     check_row = full_dot(full_check, column)
     return (result, check_row)

time: 325 us -> 344 us (1.058)
  blocking collectives: 80.2 us -> 97 us
    unnamed x0 -> x2, blocking collectives: none -> 97 us
    another operation x1 -> x0, blocking collectives: 55.8 us -> none
    psum x1 -> x0, blocking collectives: 24.4 us -> none  [multiply(): summed = lax.psum(partial_row, 'row')]
where the time goes in v1:
time: 344 us
  waiting for transfers between devices  170 us (49%)
  blocking collectives  97 us (28%)
  matrix products  58.1 us (17%)
  between operations  15.1 us (4%)
    unnamed x2, blocking collectives  97 us
    all_gather x1, waiting for transfers between devices, body(): column = lax.all_gather(current, 'row', axis=0, tiled=True)  94.3 us
    all_gather x2, waiting for transfers between devices, multiply(): lax.all_gather(left_tile, 'col', axis=1, tiled=True)  73.9 us
    dot_general x6, matrix products, full_dot(): jnp.dot(first, second, precision=lax.Precision.HIGHEST, preferred_element...  58.1 us
  transfers between devices with their start and end apart: 3, of which 2 were waited for; matrix products, arithmetic and copies ran while one was open for 6% of the time, Pallas kernels for 0%

profile of v1, /device:TPU:0, one launch (start us, length us, event | category | flops | bytes accessed | tf_op | source)
XLA Modules:
  0.0 344.0 jit_solution(11855431686685615197)
XLA Ops:
  7.2 0.0 all-gather.10.cloned.1.call-start
  7.2 0.7 all-gather.10.cloned.1.call-update
  7.9 0.0 all-gather.8.cloned.1.call-start
  7.9 0.7 all-gather.8.cloned.1.call-update
  8.6 0.0 all-gather.12.cloned.1.call-start
  8.7 0.7 convert_element_type.3
  9.4 0.1 broadcast_in_dim.7
  9.5 0.1 reshape.28
  9.5 94.3 %all-gather.10.cloned.1.call-done = f32[5120,320]{0,1:T(8,128)} async-done(((f32[640,320]{0,1:T(8,128)}), f32[5120,320]{0,1:T(8,128)}) %all-gather.10.cloned.1.call-update) | async-done | bytes 6553616 | tf_op jit(solution)/shard_map/all_gather | solution.py:33
  103.9 73.9 %all-gather.8.cloned.1.call-done = f32[640,5120]{0,1:T(8,128)} async-done(((f32[640,320]{0,1:T(8,128)}), f32[640,5120]{0,1:T(8,128)}) %all-gather.8.cloned.1.call-update) | async-done | bytes 13107216 | tf_op jit(solution)/shard_map/all_gather | solution.py:21
  177.8 0.1 broadcast_in_dim.8
  177.9 0.0 copy-start.2
  177.9 0.0 copy-start.4
  177.9 0.0 copy-start.3
  177.9 0.0 copy-start.1
  177.9 20.3 %convolution_multiply_fusion.1 = f32[640,320]{0,1:T(8,128)} fusion(f32[640,320]{0,1:T(8,128)S(1)} %bitcast.19, f32[640,5120]{0,1:T(8,128)} %all-gather.8.cloned.1.call-done, f32[5120,320]{0,1:T(8,128)} %all-gather.10.cloned.1.call-done), kind=kOutput, calls=%fused_computation.1 | convolution fusion | flops 12583116800 | bytes 21299200 | tf_op jit(solution)/shard_map/dot_general | solution.py:10
  198.2 0.0 all-gather.12.cloned.1.call-update
  198.3 0.0 copy-done.2
  198.3 0.0 copy-done.4
  198.3 0.6 dynamic-slice
  198.9 0.0 copy-done.3
  198.9 0.6 dynamic-slice.1
  200.7 0.0 copy-done.1
  200.7 0.8 convolution_reduce_fusion.1
  201.5 0.3 dynamic-update-slice
  201.8 1.9 convolution_reduce_fusion
  203.8 0.3 dynamic-update-slice.2
  204.0 42.3 %all-reduce.5 = (f32[2560]{0:T(1024)S(1)}, f32[2560]{0:T(1024)S(1)}) all-reduce(f32[2560]{0:T(1024)S(1)} %dynamic-update-slice.2, f32[2560]{0:T(1024)S(1)} %dynamic-update-slice), channel_id=4, replica_groups=mesh['row'=8,'col'=16] {'row'}, use_global_device_ids=true, to_apply=%add.2 | all-reduce | flops 5120 | bytes 40960
  246.3 0.1 reshape.32
  246.4 0.1 reshape.34
  246.5 0.3 dynamic-update-slice.1
  246.8 0.3 dynamic-update-slice.3
  247.1 54.7 %all-reduce.4 = (f32[5120]{0:T(1024)S(1)}, f32[5120]{0:T(1024)S(1)}) all-reduce(f32[5120]{0:T(1024)S(1)} %dynamic-update-slice.3, f32[5120]{0:T(1024)S(1)} %dynamic-update-slice.1), channel_id=5, replica_groups=mesh['row'=8,'col'=16] {'col'}, use_global_device_ids=true, to_apply=%add.3 | all-reduce | flops 10240 | bytes 81920
  301.8 0.0 copy-start
  301.8 7.4 %fusion.2 = f32[1,320]{1,0:T(1,128)S(1)} fusion(f32[5120,1]{0,1:T(1,128)S(1)} %bitcast.22, f32[5120,320]{0,1:T(8,128)} %all-gather.10.cloned.1.call-done), kind=kOutput, calls=%fused_computation.7 | convolution fusion | flops 19660800 | bytes 6575360 | tf_op jit(solution)/shard_map/dot_general | solution.py:10
  309.2 7.3 %fusion.3 = f32[1,320]{1,0:T(1,128)S(1)} fusion(f32[5120,1]{0,1:T(1,128)S(1)} %bitcast.21, f32[5120,320]{0,1:T(8,128)} %all-gather.10.cloned.1.call-done), kind=kOutput, calls=%fused_computation.8 | convolution fusion | flops 19660800 | bytes 6575360 | tf_op jit(solution)/shard_map/dot_general | solution.py:10
  316.5 0.6 pad_maximum_fusion
  317.1 0.0 all-gather.12.cloned.1.call-done
  317.2 0.0 copy-done
  317.2 20.3 %fusion.1 = f32[640,320]{0,1:T(8,128)} fusion(f32[640,320]{0,1:T(8,128)S(1)} %bitcast.20, f32[640,5120]{0,1:T(8,128)} %all-gather.12.cloned.1.call-done, f32[5120,320]{0,1:T(8,128)} %all-gather.10.cloned.1.call-done, f32[640,320]{0,1:T(8,128)S(1)} %copy-done), kind=kOutput, calls=%fused_computation.3 | convolution fusion | flops 12583731200 | bytes 22118400 | tf_op jit(solution)/shard_map/dot_general | solution.py:10
  (7 shorter events, 0.1 us)
Async XLA Ops:
  7.2 96.7 %all-gather.10.cloned.1.call-start = ((), (), s32[]{:S(2)}) async-start(), calls=%async_computation.1 | async-start | bytes 7372800 | tf_op jit(solution)/shard_map/all_gather | solution.py:33
  7.9 169.9 %all-gather.8.cloned.1.call-start = ((), (), s32[]{:S(2)}) async-start(), calls=%async_computation | async-start | bytes 13926400 | tf_op jit(solution)/shard_map/all_gather | solution.py:21
  8.6 308.5 %all-gather.12.cloned.1.call-start = ((), (), s32[]{:S(2)}) async-start(), calls=%async_computation.2 | async-start | bytes 13926400 | tf_op jit(solution)/shard_map/all_gather | solution.py:21
  177.9 20.4 %copy-start.2 = (f32[640]{0:T(1024)S(1)}, f32[640]{0:T(1024)}, u32[]{:S(2)}) copy-start(f32[640]{0:T(1024)} %param.5) | copy-start | bytes 7684
  177.9 20.4 %copy-start.4 = (u32[128]{0:T(128)S(1)}, u32[128]{0:T(128)}, u32[]{:S(2)}) copy-start(u32[128]{0:T(128)} %constant.9) | copy-start | bytes 1540
  177.9 21.0 %copy-start.3 = (u32[128]{0:T(128)S(1)}, u32[128]{0:T(128)}, u32[]{:S(2)}) copy-start(u32[128]{0:T(128)} %constant.14) | copy-start | bytes 1540
  177.9 22.8 %copy-start.1 = (f32[640,320]{0,1:T(8,128)S(1)}, f32[640,320]{0,1:T(8,128)}, u32[]{:S(2)}) copy-start(f32[640,320]{0,1:T(8,128)} %param.3) | copy-start | bytes 2457604
  301.8 15.4 %copy-start = (f32[640,320]{0,1:T(8,128)S(1)}, f32[640,320]{0,1:T(8,128)}, u32[]{:S(2)}) copy-start(f32[640,320]{0,1:T(8,128)} %convolution_multiply_fusion.1) | copy-start | bytes 2457604
Sparse Core Ops, SparseCore 0:
  10.3 93.5 all-gather.9
  105.6 72.1 all-gather.7
  198.4 76.9 all-gather.11

commit v2 on v0

--- a/solution.py
+++ b/solution.py
@@ -30,7 +30,9 @@
     current = density
     weight_row = weights[None, :]
     checks = []
-    column = lax.all_gather(current, "row", axis=0, tiled=True)
+    column = jnp.concatenate(
+        lax.all_to_all(jnp.stack([current] * lax.axis_size("row")), "row", 0, 0), axis=0
+    )
     square, first_check = multiply(current, column, weight_row)
     square = block_mask * square
     cube_term, second_check = multiply(square, column, weight_row)

time: 325 us -> 303 us (0.932)
  waiting for transfers between devices: 170 us -> 129 us
  local copies, waits for them, and re-layouts: 1.36 us -> 12.1 us
  starting transfers between devices: 0.11 us -> 7.25 us
    all_gather x1 -> x0, waiting for transfers between devices: 94.3 us -> none  [body(): column = lax.all_gather(current, 'row', axis=0, tiled=True)]
    all_to_all x0 -> x1, waiting for transfers between devices: none -> 91.3 us  [body(): lax.all_to_all(jnp.stack([current] * lax.axis_size('row')), 'row', 0, 0)]
    all_gather x2, waiting for transfers between devices: 73.9 us -> 36.6 us  [multiply(): lax.all_gather(left_tile, 'col', axis=1, tiled=True)]
    all_to_all x0 -> x1, starting transfers between devices: none -> 7.17 us  [body(): lax.all_to_all(jnp.stack([current] * lax.axis_size('row')), 'row', 0, 0)]
    reshape x0 -> x1, local copies, waits for them, and re-layouts: none -> 6.5 us  [body(): jnp.concatenate(lax.all_to_all(jnp.stack([current] * lax.axis_size('row')...]
    another operation x0 -> x1, local copies, waits for them, and re-layouts: none -> 4.24 us  [body(): jnp.stack([current] * lax.axis_size('row'))]
  transfers between devices with their start and end apart: 3 -> 3, of which waited for: 2 -> 2; matrix products, arithmetic and copies ran while one was open for 6% -> 10% of each run, Pallas kernels for 0% -> 0%
where the time goes in v2:
time: 303 us
  waiting for transfers between devices  129 us (43%)
  blocking collectives  81.3 us (27%)
  matrix products  58 us (19%)
  between operations  14.8 us (5%)
  local copies, waits for them, and re-layouts  12.1 us (4%)
  starting transfers between devices  7.25 us (2%)
    all_to_all x1, waiting for transfers between devices, body(): lax.all_to_all(jnp.stack([current] * lax.axis_size('row')), 'row', 0, 0)  91.3 us
    dot_general x6, matrix products, full_dot(): jnp.dot(first, second, precision=lax.Precision.HIGHEST, preferred_element...  58 us
    another operation x1, blocking collectives  56.1 us
    all_gather x2, waiting for transfers between devices, multiply(): lax.all_gather(left_tile, 'col', axis=1, tiled=True)  36.6 us
    psum x1, blocking collectives, multiply(): summed = lax.psum(partial_row, 'row')  25.2 us
    all_to_all x1, starting transfers between devices, body(): lax.all_to_all(jnp.stack([current] * lax.axis_size('row')), 'row', 0, 0)  7.17 us
    reshape x1, local copies, waits for them, and re-layouts, body(): jnp.concatenate(lax.all_to_all(jnp.stack([current] * lax.axis_size('row')...  6.5 us
  transfers between devices with their start and end apart: 3, of which 2 were waited for; matrix products, arithmetic and copies ran while one was open for 10% of the time, Pallas kernels for 0%

profile of v2, /device:TPU:0, one launch (start us, length us, event | category | flops | bytes accessed | tf_op | source)
XLA Modules:
  0.0 302.7 jit_solution(17070025526826073002)
XLA Ops:
  7.2 0.0 all-gather.3.cloned.1.call-start
  7.2 0.7 all-gather.3.cloned.1.call-update
  7.9 4.2 %stack.2 = f32[8,640,320]{1,2,0:T(8,128)} broadcast(f32[640,320]{0,1:T(8,128)} %param.3), dimensions={1,2} | broadcast | bytes 7372800 | tf_op jit(solution)/shard_map/stack | solution.py:34
  12.1 0.0 copy-start.2
  12.1 7.2 %all-to-all-start = ((f32[8,640,320]{1,2,0:T(8,128)}), f32[8,640,320]{1,2,0:T(8,128)}, u32[]{:S(2)}, u32[]{:S(2)}) async-start(f32[8,640,320]{1,2,0:T(8,128)} %stack.2), calls=%async_computation | async-start | bytes 13107200 | tf_op jit(solution)/shard_map/all_to_all | solution.py:34
  19.3 0.0 all-gather.5.cloned.1.call-start
  19.4 0.0 copy-done.2
  19.4 0.1 broadcast_in_dim.7
  19.5 0.1 reshape.29
  19.5 91.3 %all-to-all-done = f32[8,640,320]{1,2,0:T(8,128)} async-done(((f32[8,640,320]{1,2,0:T(8,128)}), f32[8,640,320]{1,2,0:T(8,128)}, u32[]{:S(2)}, u32[]{:S(2)}) %all-to-all-start) | async-done | bytes 6553632 | tf_op jit(solution)/shard_map/all_to_all | solution.py:34
  110.8 6.5 %copy.7 = f32[8,40,8,640]{3,2,0,1:T(8,128)} copy(f32[8,40,8,640]{3,2,1,0:T(8,128)} %bitcast.4) | data formatting | bytes 13107200 | tf_op jit(solution)/shard_map/reshape | solution.py:33
  117.3 36.6 %all-gather.3.cloned.1.call-done = f32[640,5120]{0,1:T(8,128)} async-done(((f32[640,320]{0,1:T(8,128)}), f32[640,5120]{0,1:T(8,128)}) %all-gather.3.cloned.1.call-update) | async-done | bytes 13107216 | tf_op jit(solution)/shard_map/all_gather | solution.py:21
  153.9 0.1 broadcast_in_dim.8
  154.0 0.0 copy-start.3
  154.0 0.0 copy-start.4
  154.0 0.0 copy-start.1
  154.0 20.3 %convolution_multiply_fusion.1 = f32[640,320]{0,1:T(8,128)} fusion(f32[640,320]{0,1:T(8,128)S(1)} %bitcast.24, f32[640,5120]{0,1:T(8,128)} %all-gather.3.cloned.1.call-done, f32[5120,320]{0,1:T(8,128)} %bitcast.20), kind=kOutput, calls=%fused_computation.1 | convolution fusion | flops 12583116800 | bytes 21299200 | tf_op jit(solution)/shard_map/dot_general | solution.py:10
  174.3 0.0 all-gather.5.cloned.1.call-update
  174.4 0.0 copy-done.3
  174.4 0.0 copy-done.4
  174.4 0.6 dynamic-slice
  175.6 0.0 copy-done.1
  175.6 0.8 fusion.2
  176.5 1.9 fusion.4
  178.3 25.2 %all-reduce.3 = (f32[1,320]{1,0:T(1,128)S(1)}, f32[1,320]{1,0:T(1,128)S(1)}) all-reduce(f32[1,320]{1,0:T(1,128)S(1)} %fusion.4, f32[1,320]{1,0:T(1,128)S(1)} %fusion.2), channel_id=1, replica_groups=mesh['row'=8,'col'=16] {'row'}, use_global_device_ids=true, to_apply=%region_1.0 | all-reduce | flops 640 | bytes 5120 | tf_op jit(solution)/shard_map/psum | solution.py:22
  203.6 0.3 dynamic-update-slice
  203.8 0.3 dynamic-update-slice.1
  204.1 56.1 %all-reduce.2 = (f32[5120]{0:T(1024)S(1)}, f32[5120]{0:T(1024)S(1)}) all-reduce(f32[5120]{0:T(1024)S(1)} %dynamic-update-slice.1, f32[5120]{0:T(1024)S(1)} %dynamic-update-slice), channel_id=1, replica_groups=mesh['row'=8,'col'=16] {'col'}, use_global_device_ids=true, to_apply=%add.1 | all-reduce | flops 10240 | bytes 81920 | tf_op jit(solution)/shard_map/reshape.12
  260.2 0.0 copy-start
  260.2 7.4 %fusion.3 = f32[1,320]{1,0:T(1,128)S(1)} fusion(f32[5120,1]{0,1:T(1,128)S(1)} %bitcast.27, f32[5120,320]{0,1:T(8,128)} %bitcast.21), kind=kOutput, calls=%fused_computation.6 | convolution fusion | flops 19660800 | bytes 6575360 | tf_op jit(solution)/shard_map/dot_general | solution.py:10
  267.6 7.3 %fusion.5 = f32[1,320]{1,0:T(1,128)S(1)} fusion(f32[5120,1]{0,1:T(1,128)S(1)} %bitcast.26, f32[5120,320]{0,1:T(8,128)} %bitcast.22), kind=kOutput, calls=%fused_computation.8 | convolution fusion | flops 19660800 | bytes 6575360 | tf_op jit(solution)/shard_map/dot_general | solution.py:10
  274.9 0.6 pad_maximum_fusion
  275.6 0.0 all-gather.5.cloned.1.call-done
  275.6 0.0 copy-done
  275.6 20.3 %fusion.1 = f32[640,320]{0,1:T(8,128)} fusion(f32[640,320]{0,1:T(8,128)S(1)} %bitcast.25, f32[640,5120]{0,1:T(8,128)} %all-gather.5.cloned.1.call-done, f32[5120,320]{0,1:T(8,128)} %bitcast.23, f32[640,320]{0,1:T(8,128)S(1)} %copy-done), kind=kOutput, calls=%fused_computation.3 | convolution fusion | flops 12583731200 | bytes 22118400 | tf_op jit(solution)/shard_map/dot_general | solution.py:10
  (6 shorter events, 0.1 us)
Async XLA Ops:
  7.2 146.7 %all-gather.3.cloned.1.call-start = ((), (), s32[]{:S(2)}) async-start(), calls=%async_computation.1 | async-start | bytes 13926400 | tf_op jit(solution)/shard_map/all_gather | solution.py:21
  12.1 7.2 %copy-start.2 = (s32[10,5]{0,1:T(8,128)S(1)}, s32[10,5]{0,1:T(8,128)}, u32[]{:S(2)}) copy-start(s32[10,5]{0,1:T(8,128)} %param.4) | copy-start | bytes 604
  12.1 98.7 %all-to-all-start = ((f32[8,640,320]{1,2,0:T(8,128)}), f32[8,640,320]{1,2,0:T(8,128)}, u32[]{:S(2)}, u32[]{:S(2)}) async-start(f32[8,640,320]{1,2,0:T(8,128)} %stack.2), calls=%async_computation | async-start | bytes 13107200 | tf_op jit(solution)/shard_map/all_to_all | solution.py:34
  19.3 256.2 %all-gather.5.cloned.1.call-start = ((), (), s32[]{:S(2)}) async-start(), calls=%async_computation.2 | async-start | bytes 13926400 | tf_op jit(solution)/shard_map/all_gather | solution.py:21
  154.0 20.4 %copy-start.3 = (f32[640]{0:T(1024)S(1)}, f32[640]{0:T(1024)}, u32[]{:S(2)}) copy-start(f32[640]{0:T(1024)} %param.5) | copy-start | bytes 7684
  154.0 20.4 %copy-start.4 = (u32[128]{0:T(128)S(1)}, u32[128]{0:T(128)}, u32[]{:S(2)}) copy-start(u32[128]{0:T(128)} %constant.7) | copy-start | bytes 1540
  154.0 21.6 %copy-start.1 = (f32[640,320]{0,1:T(8,128)S(1)}, f32[640,320]{0,1:T(8,128)}, u32[]{:S(2)}) copy-start(f32[640,320]{0,1:T(8,128)} %param.3) | copy-start | bytes 2457604
  260.2 15.4 %copy-start = (f32[640,320]{0,1:T(8,128)S(1)}, f32[640,320]{0,1:T(8,128)}, u32[]{:S(2)}) copy-start(f32[640,320]{0,1:T(8,128)} %convolution_multiply_fusion.1) | copy-start | bytes 2457604
Sparse Core Ops, SparseCore 0:
  9.7 144.1 all-gather.2
  174.5 78.8 all-gather.4
